TPU v7x, 512 devices: a whole 4x8x8 slice. The times are simulated.
512 devices in a mesh: req: 64 (over z, x, core), mdl: 8 (over y).
Axes of the slice: x: 4, y: 8, z: 8, core: 2. Of those that a mesh axis runs over, the one named last changes fastest.
Arguments:
- hidden_in: bfloat16 [8192, 2048], P('req'), may hold values from -6 to 6
- z_weight: bfloat16 [2048, 4096], P('req', 'mdl'), may hold values from -0.125 to 0.125
- x_weight: bfloat16 [2048, 4096], P('req', 'mdl'), may hold values from -0.125 to 0.125
- state_proj: bfloat16 [2048, 256], P('req'), may hold values from -0.125 to 0.125
- step_weight: bfloat16 [2048, 64], P('req', 'mdl'), may hold values from -0.125 to 0.125
- step_bias: float32 [64], P('mdl'), may hold values from -4 to -1
- decay_log: float32 [64], P('mdl'), may hold values from -2 to 1
- skip_gain: float32 [64], P('mdl'), may hold values from 0.5 to 2
- conv_inner: float32 [4, 4096], P(None, 'mdl'), may hold values from -3 to 3
- conv_state: float32 [4, 256], replicated, may hold values from -3 to 3
- norm_gain: float32 [4096], P('mdl'), may hold values from 0.1 to 1.9
- out_weight: bfloat16 [4096, 2048], P('mdl', 'req'), may hold values from -0.09375 to 0.09375
- state_pool: float32 [512, 64, 64, 128], P('req', 'mdl'), may hold values from -2.4 to 2.4
- conv_pool_inner: bfloat16 [512, 3, 4096], P('req', None, 'mdl'), may hold values from -6 to 6
- conv_pool_state: bfloat16 [512, 3, 256], P('req'), may hold values from -6 to 6
- owner_dev: int32 [512], replicated, may hold values from 0 to 63, as said below
- state_page: int32 [512], replicated, may hold values from 0 to 7, as said below
- conv_page: int32 [512], replicated, may hold values from 0 to 7, as said below
- accepted: int32 [512], replicated, may hold values from 1 to 16
Outputs:
- mixed: bfloat16 [8192, 2048], P('req', 'mdl')
- new_states: float32 [512, 64, 64, 128], P('req', 'mdl')
- conv_inner_out: bfloat16 [512, 3, 4096], P('req', None, 'mdl')
- conv_state_out: bfloat16 [512, 3, 256], P('req')
Inputs may be any that keep to these rules, and one draw needn't show every extreme that they name: `owner_dev`: request r of device i = r // 8 has its owner among devices i to i + 7 along req, counted modulo the axis size; among the 8 requests of one device at most 2 name the same owner, and exactly 2 do for one owner; every owner is named by exactly 8 requests in all. `state_page`: the requests of one owner have distinct state slots. `conv_page`: the requests of one owner have distinct convolution pages.
All inputs are finite; a program needn't handle non-finite values.
Results may differ from a plain program's by a relative error of at most 0.0069.
Values may be sent and summed in bfloat16 or wider, within the bound.
A program may use at most 64 MiB of HBM per device.

v0:
```python
import jax
import jax.numpy as jnp
from jax import lax
from jax.sharding import PartitionSpec as P

KCONV = 4
CAP = 2
WINDOW = 8
HIGH = lax.Precision.HIGHEST
EPSILON = 1e-05


def from_behind(value, axis, steps):
    count = lax.axis_size(axis)
    pairs = [(source, (source + steps) % count) for source in range(count)]
    return lax.ppermute(value, axis, pairs)


def one_hot_apply(table, values, shape):
    flat = values.reshape(table.shape[1], -1)
    return (
        jnp.dot(table, flat, preferred_element_type=jnp.float32).astype(jnp.bfloat16).reshape(shape)
    )


def route_tables(owner_dev, state_page, conv_page, accepted, groups, per_dev, this_dev):
    owner_grid = owner_dev.reshape(groups, per_dev)
    home_grid = jnp.arange(groups, dtype=jnp.int32)[:, None]
    offset_grid = (owner_grid - home_grid + groups) % groups
    positions = jnp.arange(per_dev, dtype=jnp.int32)
    earlier = positions[None, :] < positions[:, None]
    pair_rank = jnp.sum((owner_grid[:, :, None] == owner_grid[:, None, :]) & earlier[None], axis=2)
    slot_grid = offset_grid * CAP + pair_rank
    send_at = lax.dynamic_slice_in_dim(slot_grid, this_dev, 1, 0)[0]
    buffer_rows = jnp.arange(WINDOW * CAP, dtype=jnp.int32)
    send_table = (buffer_rows[:, None] == send_at[None, :]).astype(jnp.bfloat16)
    arrive_at = slot_grid.reshape(-1)
    slot_match = (owner_dev[None, :] == this_dev) & (state_page[None, :] == positions[:, None])
    pick_from = jnp.sum(jnp.where(slot_match, arrive_at[None, :], 0), axis=1)
    conv_of = jnp.sum(jnp.where(slot_match, conv_page[None, :], 0), axis=1)
    kept_count = jnp.sum(jnp.where(slot_match, accepted[None, :], 0), axis=1)
    gather_table = (buffer_rows[None, :] == pick_from[:, None]).astype(jnp.bfloat16)
    place_table = (positions[:, None] == conv_of[None, :]).astype(jnp.bfloat16)
    return (send_table, gather_table, place_table, conv_of, kept_count)


def project_in(rows, z_weight, x_weight, state_proj, step_weight):
    pieces = (
        lax.all_gather(z_weight, "req", axis=0, tiled=True),
        lax.all_gather(x_weight, "req", axis=0, tiled=True),
        lax.all_gather(state_proj, "req", axis=0, tiled=True),
        lax.all_gather(step_weight, "req", axis=0, tiled=True),
    )
    gate_pre, inner_raw, state_full, step_raw = tuple(
        (jnp.dot(rows, piece, preferred_element_type=jnp.float32) for piece in pieces)
    )
    state_raw = state_full.astype(jnp.bfloat16)
    packed = jnp.concatenate([inner_raw.astype(jnp.bfloat16), state_raw], axis=1)
    return (gate_pre, packed, step_raw.astype(jnp.bfloat16))


def mix_requests(
    packed, step_raw, history, kernel, step_bias, decay_log, skip_gain, state_pool, kept_count
):
    per_dev, draft, channels = packed.shape
    heads, head_dim, state_width = (state_pool.shape[1], state_pool.shape[2], state_pool.shape[3])
    inner = heads * head_dim
    series = jnp.concatenate([history, packed], axis=1)
    series_f = series.astype(jnp.float32)
    conv_sum = kernel[0] * series_f[:, 0:draft]
    for tap in range(1, KCONV):
        conv_sum = conv_sum + kernel[tap] * series_f[:, tap : tap + draft]
    active = jax.nn.silu(conv_sum)
    inputs_x = active[:, :, :inner].reshape(per_dev, draft, heads, head_dim)
    b_rows = active[:, :, inner : inner + state_width]
    c_rows = active[:, :, inner + state_width :]
    step_size = jax.nn.softplus(step_raw.astype(jnp.float32) + step_bias)
    log_decay = jnp.cumsum(step_size * -jnp.exp(decay_log), axis=1)
    step_order = jnp.arange(draft, dtype=jnp.int32)
    causal = (step_order[None, :] <= step_order[:, None])[None, :, :, None]
    spread = log_decay[:, :, None, :] - log_decay[:, None, :, :]
    decay_table = jnp.where(causal, jnp.exp(jnp.where(causal, spread, 0.0)), 0.0)
    scores = jnp.einsum("stn,sun->stu", c_rows, b_rows, precision=HIGH)
    weights = decay_table * scores[:, :, :, None] * step_size[:, None, :, :]
    within = jnp.einsum("stuh,suhp->sthp", weights, inputs_x, precision=HIGH)
    carried = (
        jnp.einsum("stn,shpn->sthp", c_rows, state_pool, precision=HIGH)
        * jnp.exp(log_decay)[:, :, :, None]
    )
    outputs = within + carried + skip_gain[:, None] * inputs_x
    at_end = (step_order[None, :] == (kept_count - 1)[:, None])[:, :, None]
    end_decay = jnp.sum(jnp.where(at_end, log_decay, 0.0), axis=1)
    before = (step_order[None, :] < kept_count[:, None])[:, :, None]
    gap = end_decay[:, None, :] - log_decay
    select_weight = jnp.where(before, jnp.exp(jnp.where(before, gap, 0.0)), 0.0) * step_size
    chosen = jnp.exp(end_decay)[:, :, None, None] * state_pool + jnp.einsum(
        "suh,suhp,sun->shpn", select_weight, inputs_x, b_rows, precision=HIGH
    )
    series_rows = jnp.arange(series.shape[1], dtype=jnp.int32)
    window = (
        series_rows[None, None, :]
        == kept_count[:, None, None] + jnp.arange(KCONV - 1, dtype=jnp.int32)[None, :, None]
    ).astype(jnp.bfloat16)
    edge_rows = jnp.einsum(
        "sir,src->sic", window, series, preferred_element_type=jnp.float32
    ).astype(jnp.bfloat16)
    return (outputs.reshape(per_dev, draft, inner).astype(jnp.bfloat16), chosen, edge_rows)


def finish(mixed_rows, gate_pre, norm_gain, out_weight):
    gated = mixed_rows.astype(jnp.float32) * jax.nn.silu(gate_pre)
    inner_total = gated.shape[1] * lax.axis_size("mdl")
    squares = lax.psum(jnp.sum(gated * gated, axis=1), "mdl")
    normed = (gated * lax.rsqrt(squares[:, None] / inner_total + EPSILON) * norm_gain).astype(
        jnp.bfloat16
    )
    terms = jnp.dot(
        normed,
        lax.all_gather(out_weight, "req", axis=1, tiled=True),
        preferred_element_type=jnp.float32,
    )
    return lax.psum_scatter(terms, "mdl", scatter_dimension=1, tiled=True).astype(jnp.bfloat16)


def on_device(
    hidden_in,
    z_weight,
    x_weight,
    state_proj,
    step_weight,
    step_bias,
    decay_log,
    skip_gain,
    conv_inner,
    conv_state,
    norm_gain,
    out_weight,
    state_pool,
    conv_pool_inner,
    conv_pool_state,
    owner_dev,
    state_page,
    conv_page,
    accepted,
):
    groups = lax.axis_size("req")
    this_dev = lax.axis_index("req")
    per_dev = state_pool.shape[0]
    draft = hidden_in.shape[0] // per_dev
    slots = WINDOW * CAP
    send_table, gather_table, place_table, conv_of, kept_count = route_tables(
        owner_dev, state_page, conv_page, accepted, groups, per_dev, this_dev
    )
    history = jnp.concatenate([conv_pool_inner[conv_of], conv_pool_state[conv_of]], axis=2)
    kernel = jnp.concatenate([conv_inner, conv_state], axis=1)
    gate_pre, packed, step_raw = project_in(hidden_in, z_weight, x_weight, state_proj, step_weight)
    channels = packed.shape[1]
    payload = jnp.concatenate([packed, step_raw], axis=1)
    total_cols = payload.shape[1]
    outgoing = one_hot_apply(send_table, payload, (slots, draft, total_cols))
    incoming = jnp.concatenate(
        [
            from_behind(outgoing[offset * CAP : (offset + 1) * CAP], "req", offset)
            for offset in range(WINDOW)
        ],
        axis=0,
    )
    owned = one_hot_apply(gather_table, incoming, (per_dev, draft, total_cols))
    mixed_rows, chosen, edge_rows = mix_requests(
        owned[:, :, :channels],
        owned[:, :, channels:],
        history,
        kernel,
        step_bias,
        decay_log,
        skip_gain,
        state_pool,
        kept_count,
    )
    inner_local = mixed_rows.shape[2]
    returning = one_hot_apply(gather_table.T, mixed_rows, (slots, draft, inner_local))
    arrived = jnp.concatenate(
        [
            from_behind(returning[offset * CAP : (offset + 1) * CAP], "req", -offset)
            for offset in range(WINDOW)
        ],
        axis=0,
    )
    home_rows = one_hot_apply(send_table.T, arrived, (per_dev * draft, inner_local))
    mixed = finish(home_rows, gate_pre, norm_gain, out_weight)
    placed = one_hot_apply(place_table, edge_rows, edge_rows.shape)
    inner_cols = conv_pool_inner.shape[2]
    return (mixed, chosen, placed[:, :, :inner_cols], placed[:, :, inner_cols:])


def solution(mesh):
    return jax.shard_map(
        on_device,
        mesh=mesh,
        in_specs=(
            P("req", None),
            P("req", "mdl"),
            P("req", "mdl"),
            P("req", None),
            P("req", "mdl"),
            P("mdl"),
            P("mdl"),
            P("mdl"),
            P(None, "mdl"),
            P(),
            P("mdl"),
            P("mdl", "req"),
            P("req", "mdl", None, None),
            P("req", None, "mdl"),
            P("req", None, None),
            P(),
            P(),
            P(),
            P(),
        ),
        out_specs=(
            P("req", "mdl"),
            P("req", "mdl", None, None),
            P("req", None, "mdl"),
            P("req", None, None),
        ),
        check_vma=False,
    )
```

profile of v0, /device:TPU:4, one launch (start us, length us, event | category | flops | bytes accessed | tf_op | source)
XLA Modules:
  0.0 400.5 jit_solution(18413724058797244592)
XLA Ops:
  10.0 0.8 reshape.219
  12.7 0.9 select_reduce_fusion.1
  14.8 55.4 %all-gather = bf16[64,32,8]{1,2,0:T(8,128)(2,1)S(1)} all-gather(bf16[1,32,8]{1,2,0:T(8,128)(2,1)} %bitcast.102), channel_id=1, replica_groups=mesh['req'=64,'mdl'=8] {'req'}, dimensions={0}, use_global_device_ids=true | all-gather | bytes 33280 | tf_op jit(solution)/shard_map/all_gather | solution.py:52
  73.0 24.6 %all-gather.8.cloned.1.call-done = bf16[2048,256]{1,0:T(8,128)(2,1)} async-done(((bf16[32,256]{1,0:T(8,128)(2,1)}), bf16[2048,256]{1,0:T(8,128)(2,1)}) %all-gather.8.cloned.1.call-update) | async-done | bytes 1048592 | tf_op jit(solution)/shard_map/all_gather | solution.py:51
  97.6 1.5 convolution_convert_fusion.6
  99.2 82.5 %all-gather.6.cloned.1.call-done = bf16[2048,512]{1,0:T(8,128)(2,1)} async-done(((bf16[32,512]{1,0:T(8,128)(2,1)}), bf16[2048,512]{1,0:T(8,128)(2,1)}) %all-gather.6.cloned.1.call-update) | async-done | bytes 2097168 | tf_op jit(solution)/shard_map/all_gather | solution.py:50
  181.7 2.0 convolution_convert_fusion.5
  186.8 2.2 collective-permute-start.1
  189.2 3.1 collective-permute-start.2
  192.4 3.3 collective-permute-start.3
  195.9 3.3 collective-permute-start.4
  199.7 4.5 %collective-permute-start.5 = (bf16[2,16,776]{2,1,0:T(8,128)(2,1)S(1)}, bf16[2,16,776]{2,1,0:T(8,128)(2,1)S(1)}, u32[]{:S(2)}, u32[]{:S(2)}) collective-permute-start(bf16[2,16,776]{2,1,0:T(8,128)(2,1)S(1)} %slice.153), channel_id=1, source_target_pairs={{0,40},{8,48},{16,56},{24,64},{32,72},{40,80},{48,88},{56,96},{64,... | collective-permute-start | bytes 149000 | tf_op jit(solution)/shard_map/ppermute | solution.py:16
  204.2 4.1 %collective-permute-start.6 = (bf16[2,16,776]{2,1,0:T(8,128)(2,1)S(1)}, bf16[2,16,776]{2,1,0:T(8,128)(2,1)S(1)}, u32[]{:S(2)}, u32[]{:S(2)}) collective-permute-start(bf16[2,16,776]{2,1,0:T(8,128)(2,1)S(1)} %slice.155), channel_id=1, source_target_pairs={{0,48},{8,56},{16,64},{24,72},{32,80},{40,88},{48,96},{56,104},{64... | collective-permute-start | bytes 149000 | tf_op jit(solution)/shard_map/ppermute | solution.py:16
  208.3 3.9 collective-permute-start.7
  212.4 2.6 collective-permute-done.7
  218.2 0.7 slice.209
  218.9 0.9 fusion.29
  220.4 1.1 reshape.223
  221.6 5.8 %convolution_multiply_fusion = f32[8,16,8,64]{3,1,2,0:T(8,128)S(1)} fusion(f32[8,8,64,128]{3,2,1,0:T(8,128)S(1)} %copy-done.1, f32[8,16,8]{1,2,0:T(8,128)} %copy.138, f32[8,16,768]{2,1,0:T(8,128)S(1)} %divide_multiply_fusion), kind=kOutput, calls=%fused_computation.9 | convolution fusion | flops 100728832 | bytes 2428928 | tf_op jit(solution)/shard_map/stn,shpn->sthp/dot_general | solution.py:87
  228.2 0.9 fusion.3
  229.1 0.8 copy.140
  229.9 1.9 convert_element_type.68
  231.7 1.2 convolution_convert_fusion.2
  233.2 3.8 collective-permute-start.9
  237.0 2.1 collective-permute-start.10
  239.2 2.8 collective-permute-start.11
  241.9 4.8 %collective-permute-start.12 = (bf16[2,16,512]{2,1,0:T(8,128)(2,1)S(1)}, bf16[2,16,512]{2,1,0:T(8,128)(2,1)S(1)}, u32[]{:S(2)}, u32[]{:S(2)}) collective-permute-start(bf16[2,16,512]{2,1,0:T(8,128)(2,1)S(1)} %bitcast.97), channel_id=1, source_target_pairs={{0,480},{8,488},{16,496},{24,504},{32,0},{40,8},{48,16},{56,24},{6... | collective-permute-start | bytes 98312 | tf_op jit(solution)/shard_map/ppermute | solution.py:16
  246.8 2.4 collective-permute-start.13
  249.2 4.7 %collective-permute-start.14 = (bf16[2,16,512]{2,1,0:T(8,128)(2,1)S(1)}, bf16[2,16,512]{2,1,0:T(8,128)(2,1)S(1)}, u32[]{:S(2)}, u32[]{:S(2)}) collective-permute-start(bf16[2,16,512]{2,1,0:T(8,128)(2,1)S(1)} %bitcast.95), channel_id=1, source_target_pairs={{0,464},{8,472},{16,480},{24,488},{32,496},{40,504},{48,0},{56,8},... | collective-permute-start | bytes 98312 | tf_op jit(solution)/shard_map/ppermute | solution.py:16
  253.9 1.9 collective-permute-start.15
  255.9 0.7 collective-permute-done.14
  256.7 3.4 collective-permute-done.15
  260.2 0.9 fusion
  261.2 1.7 reshape.227
  262.9 2.7 all-gather.10.cloned.1.call-done
  265.6 2.7 multiply_reduce_fusion
  268.4 17.2 %psum.7 = f32[128]{0:T(128)S(1)} all-reduce(f32[128]{0:T(128)S(1)} %get-tuple-element.29), channel_id=1, replica_groups=mesh['req'=64,'mdl'=8] {'mdl'}, use_global_device_ids=true, to_apply=%region_5.6 | all-reduce | flops 128 | bytes 1024 | tf_op jit(solution)/shard_map/psum | solution.py:113
  286.1 63.5 %all-gather.12.cloned.1.call-done = bf16[512,2048]{0,1:T(8,128)(2,1)} async-done(((bf16[512,32]{0,1:T(8,128)(2,1)}), bf16[512,2048]{0,1:T(8,128)(2,1)}) %all-gather.12.cloned.1.call-update) | async-done | bytes 2097168 | tf_op jit(solution)/shard_map/all_gather | solution.py:119
  349.6 3.6 fusion.23
  353.2 0.7 iota_add_fusion
  353.9 1.3 exp.41
  355.2 1.2 fusion.4
  356.4 0.7 convolution_convert_fusion.4
  358.3 1.5 copy.143
  359.8 1.0 broadcast_multiply_fusion
  360.8 5.6 %multiply_add_fusion = f32[8,8,64,128]{3,2,1,0:T(8,128)} fusion(f32[8,8,64,128]{3,2,1,0:T(8,128)S(1)} %copy-done.1, f32[8,8]{1,0:T(8,128)} %exp.41, f32[8,16,8,64]{3,2,1,0:T(8,128)S(1)} %broadcast_multiply_fusion, f32[8,16,768]{2,1,0:T(8,128)S(1)} %divide_multiply_fusion), kind=kOutput, calls=%fused_computation.8 | convolution fusion | flops 101711872 | bytes 4784384 | tf_op jit(solution)/shard_map/suh,suhp,sun->shpn/dot_general | solution.py:96
  366.5 26.0 %reduce-scatter.2.cloned.1.call-done = f32[128,256]{1,0:T(8,128)} async-done(((f32[128,2048]{1,0:T(8,128)}), f32[128,256]{1,0:T(8,128)}) %reduce-scatter.2.cloned.1.call-update) | async-done | bytes 131088 | tf_op jit(solution)/shard_map/reduce_scatter | solution.py:122
  392.4 1.5 convert_element_type.74
  (156 shorter events, 19.7 us)
Async XLA Ops:
  7.2 63.2 %copy-start = (bf16[128,2048]{1,0:T(8,128)(2,1)S(1)}, bf16[128,2048]{1,0:T(8,128)(2,1)}, u32[]{:S(2)}) copy-start(bf16[128,2048]{1,0:T(8,128)(2,1)} %param.19) | copy-start | bytes 1572868
  7.2 90.4 %all-gather.8.cloned.1.call-start = ((), (), s32[]{:S(2)}) async-start(), calls=%async_computation.2 | async-start | bytes 1064960 | tf_op jit(solution)/shard_map/all_gather | solution.py:51
  7.9 173.8 %all-gather.6.cloned.1.call-start = ((), (), s32[]{:S(2)}) async-start(), calls=%async_computation.1 | async-start | bytes 2129920 | tf_op jit(solution)/shard_map/all_gather | solution.py:50
  8.7 256.9 %all-gather.10.cloned.1.call-start = ((), (), s32[]{:S(2)}) async-start(), calls=%async_computation.3 | async-start | bytes 2129920 | tf_op jit(solution)/shard_map/all_gather | solution.py:49
  9.4 340.2 %all-gather.12.cloned.1.call-start = ((), (), s32[]{:S(2)}) async-start(), calls=%async_computation.4 | async-start | bytes 2129920 | tf_op jit(solution)/shard_map/all_gather | solution.py:119
  10.0 382.5 %reduce-scatter.2.cloned.1.call-start = ((), (), s32[]{:S(2)}) async-start(), calls=%async_computation.5 | async-start | bytes 1179648 | tf_op jit(solution)/shard_map/reduce_scatter | solution.py:122
  13.5 168.2 %copy-start.16 = (s32[8]{0:T(128)}, s32[8]{0:T(128)S(1)}, u32[]{:S(2)}) copy-start(s32[8]{0:T(128)S(1)} %get-tuple-element.9) | copy-start | bytes 100
  13.5 168.1 %copy-start.17 = (s32[8]{0:T(128)}, s32[8]{0:T(128)S(1)}, u32[]{:S(2)}) copy-start(s32[8]{0:T(128)S(1)} %get-tuple-element.8) | copy-start | bytes 100
  13.5 202.0 %copy-start.13 = (s32[8]{0:T(128)}, s32[8]{0:T(128)S(1)}, u32[]{:S(2)}) copy-start(s32[8]{0:T(128)S(1)} %get-tuple-element.10) | copy-start | bytes 100
  73.0 111.0 %copy-start.11 = (s32[8]{0:T(128)}, s32[8]{0:T(128)S(1)}, u32[]{:S(2)}) copy-start(s32[8]{0:T(128)S(1)} %dynamic-slice_reduce_fusion) | copy-start | bytes 100
  99.2 86.2 %copy-start.3 = (bf16[8,3,256]{2,0,1:T(8,128)(2,1)S(1)}, bf16[8,3,256]{2,0,1:T(8,128)(2,1)}, u32[]{:S(2)}) copy-start(bf16[8,3,256]{2,0,1:T(8,128)(2,1)} %param.33) | copy-start | bytes 36868
  99.2 86.8 %copy-start.2 = (bf16[8,3,512]{2,0,1:T(8,128)(2,1)S(1)}, bf16[8,3,512]{2,0,1:T(8,128)(2,1)}, u32[]{:S(2)}) copy-start(bf16[8,3,512]{2,0,1:T(8,128)(2,1)} %param.32) | copy-start | bytes 73732
  184.7 15.0 %collective-permute-start = (bf16[2,16,776]{2,1,0:T(8,128)(2,1)S(1)}, bf16[2,16,776]{2,1,0:T(8,128)(2,1)S(1)}, u32[]{:S(2)}, u32[]{:S(2)}) collective-permute-start(bf16[2,16,776]{2,1,0:T(8,128)(2,1)S(1)} %slice.143), channel_id=1, source_target_pairs={{0,0},{8,8},{16,16},{24,24},{32,32},{40,40},{48,48},{56,56},{64,64... | collective-permute-start | bytes 149000 | tf_op jit(solution)/shard_map/ppermute | solution.py:16
  186.0 31.9 %copy-start.8 = (bf16[8,3,256]{2,1,0:T(4,128)(2,1)}, bf16[8,3,256]{2,1,0:T(4,128)(2,1)S(1)}, u32[]{:S(2)}) copy-start(bf16[8,3,256]{2,1,0:T(4,128)(2,1)S(1)} %copy.130) | copy-start | bytes 36868
  186.6 29.6 %copy-start.14 = (f32[8]{0:T(128)S(1)}, f32[8]{0:T(128)}, u32[]{:S(2)}) copy-start(f32[8]{0:T(128)} %param.24) | copy-start | bytes 100
  186.6 31.2 %copy-start.6 = (bf16[8,3,512]{2,1,0:T(4,128)(2,1)}, bf16[8,3,512]{2,1,0:T(4,128)(2,1)S(1)}, u32[]{:S(2)}) copy-start(bf16[8,3,512]{2,1,0:T(4,128)(2,1)S(1)} %copy.129) | copy-start | bytes 73732
  186.8 17.4 %collective-permute-start.1 = (bf16[2,16,776]{2,1,0:T(8,128)(2,1)S(1)}, bf16[2,16,776]{2,1,0:T(8,128)(2,1)S(1)}, u32[]{:S(2)}, u32[]{:S(2)}) collective-permute-start(bf16[2,16,776]{2,1,0:T(8,128)(2,1)S(1)} %slice.145), channel_id=1, source_target_pairs={{0,8},{8,16},{16,24},{24,32},{32,40},{40,48},{48,56},{56,64},{64,7... | collective-permute-start | bytes 149000 | tf_op jit(solution)/shard_map/ppermute | solution.py:16
  189.2 19.1 %collective-permute-start.2 = (bf16[2,16,776]{2,1,0:T(8,128)(2,1)S(1)}, bf16[2,16,776]{2,1,0:T(8,128)(2,1)S(1)}, u32[]{:S(2)}, u32[]{:S(2)}) collective-permute-start(bf16[2,16,776]{2,1,0:T(8,128)(2,1)S(1)} %slice.147), channel_id=1, source_target_pairs={{0,16},{8,24},{16,32},{24,40},{32,48},{40,56},{48,64},{56,72},{64,... | collective-permute-start | bytes 149000 | tf_op jit(solution)/shard_map/ppermute | solution.py:16
  192.4 19.8 %collective-permute-start.3 = (bf16[2,16,776]{2,1,0:T(8,128)(2,1)S(1)}, bf16[2,16,776]{2,1,0:T(8,128)(2,1)S(1)}, u32[]{:S(2)}, u32[]{:S(2)}) collective-permute-start(bf16[2,16,776]{2,1,0:T(8,128)(2,1)S(1)} %slice.149), channel_id=1, source_target_pairs={{0,24},{8,32},{16,40},{24,48},{32,56},{40,64},{48,72},{56,80},{64,... | collective-permute-start | bytes 149000 | tf_op jit(solution)/shard_map/ppermute | solution.py:16
  195.9 16.4 %collective-permute-start.4 = (bf16[2,16,776]{2,1,0:T(8,128)(2,1)S(1)}, bf16[2,16,776]{2,1,0:T(8,128)(2,1)S(1)}, u32[]{:S(2)}, u32[]{:S(2)}) collective-permute-start(bf16[2,16,776]{2,1,0:T(8,128)(2,1)S(1)} %slice.151), channel_id=1, source_target_pairs={{0,32},{8,40},{16,48},{24,56},{32,64},{40,72},{48,80},{56,88},{64,... | collective-permute-start | bytes 149000 | tf_op jit(solution)/shard_map/ppermute | solution.py:16
  199.7 12.6 %collective-permute-start.5 = (bf16[2,16,776]{2,1,0:T(8,128)(2,1)S(1)}, bf16[2,16,776]{2,1,0:T(8,128)(2,1)S(1)}, u32[]{:S(2)}, u32[]{:S(2)}) collective-permute-start(bf16[2,16,776]{2,1,0:T(8,128)(2,1)S(1)} %slice.153), channel_id=1, source_target_pairs={{0,40},{8,48},{16,56},{24,64},{32,72},{40,80},{48,88},{56,96},{64,... | collective-permute-start | bytes 149000 | tf_op jit(solution)/shard_map/ppermute | solution.py:16
  204.2 8.2 %collective-permute-start.6 = (bf16[2,16,776]{2,1,0:T(8,128)(2,1)S(1)}, bf16[2,16,776]{2,1,0:T(8,128)(2,1)S(1)}, u32[]{:S(2)}, u32[]{:S(2)}) collective-permute-start(bf16[2,16,776]{2,1,0:T(8,128)(2,1)S(1)} %slice.155), channel_id=1, source_target_pairs={{0,48},{8,56},{16,64},{24,72},{32,80},{40,88},{48,96},{56,104},{64... | collective-permute-start | bytes 149000 | tf_op jit(solution)/shard_map/ppermute | solution.py:16
  208.3 6.7 %collective-permute-start.7 = (bf16[2,16,776]{2,1,0:T(8,128)(2,1)S(1)}, bf16[2,16,776]{2,1,0:T(8,128)(2,1)S(1)}, u32[]{:S(2)}, u32[]{:S(2)}) collective-permute-start(bf16[2,16,776]{2,1,0:T(8,128)(2,1)S(1)} %slice.157), channel_id=1, source_target_pairs={{0,56},{8,64},{16,72},{24,80},{32,88},{40,96},{48,104},{56,112},{6... | collective-permute-start | bytes 149000 | tf_op jit(solution)/shard_map/ppermute | solution.py:16
  216.1 1.8 copy-start.4
  217.8 3.7 copy-start.1
  221.5 5.8 %copy-start.5 = (f32[8,16,8]{1,2,0:T(8,128)S(1)}, f32[8,16,8]{1,2,0:T(8,128)}, u32[]{:S(2)}) copy-start(f32[8,16,8]{1,2,0:T(8,128)} %copy.135) | copy-start | bytes 12292
  221.5 5.8 %copy-start.20 = (pred[8,16]{1,0:T(8,128)(4,1)S(1)}, pred[8,16]{1,0:T(8,128)(4,1)}, u32[]{:S(2)}) copy-start(pred[8,16]{1,0:T(8,128)(4,1)} %iota_compare_fusion.9) | copy-start | bytes 388
  221.5 5.9 %copy-start.15 = (f32[8]{0:T(128)S(1)}, f32[8]{0:T(128)}, u32[]{:S(2)}) copy-start(f32[8]{0:T(128)} %param.24) | copy-start | bytes 100
  221.6 5.9 %copy-start.19 = (pred[8,16]{1,0:T(8,128)(4,1)S(1)}, pred[8,16]{1,0:T(8,128)(4,1)}, u32[]{:S(2)}) copy-start(pred[8,16]{1,0:T(8,128)(4,1)} %iota_compare_fusion.8) | copy-start | bytes 388
  221.6 6.6 %copy-start.7 = (f32[8,16,16]{2,1,0:T(8,128)S(1)}, f32[8,16,16]{2,1,0:T(8,128)}, u32[]{:S(2)}) copy-start(f32[8,16,16]{2,1,0:T(8,128)} %fusion.29) | copy-start | bytes 24580
  221.6 6.6 %copy-start.18 = (pred[16,16]{1,0:T(8,128)(4,1)S(1)}, pred[16,16]{1,0:T(8,128)(4,1)}, u32[]{:S(2)}) copy-start(pred[16,16]{1,0:T(8,128)(4,1)} %iota_compare_fusion.3) | copy-start | bytes 772
  221.6 6.6 %copy-start.21 = (f32[8]{0:T(128)S(1)}, f32[8]{0:T(128)}, u32[]{:S(2)}) copy-start(f32[8]{0:T(128)} %param.26) | copy-start | bytes 100
  227.5 0.7 copy-start.10
  229.1 31.1 %copy-start.12 = (s32[8]{0:T(128)S(1)}, s32[8]{0:T(128)}, u32[]{:S(2)}) copy-start(s32[8]{0:T(128)} %copy-done.11) | copy-start | bytes 100
  233.2 13.6 %collective-permute-start.8 = (bf16[2,16,512]{2,1,0:T(8,128)(2,1)S(1)}, bf16[2,16,512]{2,1,0:T(8,128)(2,1)S(1)}, u32[]{:S(2)}, u32[]{:S(2)}) collective-permute-start(bf16[2,16,512]{2,1,0:T(8,128)(2,1)S(1)} %bitcast.101), channel_id=1, source_target_pairs={{0,0},{8,8},{16,16},{24,24},{32,32},{40,40},{48,48},{56,56},{64,64... | collective-permute-start | bytes 98312 | tf_op jit(solution)/shard_map/ppermute | solution.py:16
  233.2 16.0 %collective-permute-start.9 = (bf16[2,16,512]{2,1,0:T(8,128)(2,1)S(1)}, bf16[2,16,512]{2,1,0:T(8,128)(2,1)S(1)}, u32[]{:S(2)}, u32[]{:S(2)}) collective-permute-start(bf16[2,16,512]{2,1,0:T(8,128)(2,1)S(1)} %bitcast.100), channel_id=1, source_target_pairs={{0,504},{8,0},{16,8},{24,16},{32,24},{40,32},{48,40},{56,48},{64,5... | collective-permute-start | bytes 98312 | tf_op jit(solution)/shard_map/ppermute | solution.py:16
  237.0 16.9 %collective-permute-start.10 = (bf16[2,16,512]{2,1,0:T(8,128)(2,1)S(1)}, bf16[2,16,512]{2,1,0:T(8,128)(2,1)S(1)}, u32[]{:S(2)}, u32[]{:S(2)}) collective-permute-start(bf16[2,16,512]{2,1,0:T(8,128)(2,1)S(1)} %bitcast.99), channel_id=1, source_target_pairs={{0,496},{8,504},{16,0},{24,8},{32,16},{40,24},{48,32},{56,40},{64,... | collective-permute-start | bytes 98312 | tf_op jit(solution)/shard_map/ppermute | solution.py:16
  239.2 16.7 %collective-permute-start.11 = (bf16[2,16,512]{2,1,0:T(8,128)(2,1)S(1)}, bf16[2,16,512]{2,1,0:T(8,128)(2,1)S(1)}, u32[]{:S(2)}, u32[]{:S(2)}) collective-permute-start(bf16[2,16,512]{2,1,0:T(8,128)(2,1)S(1)} %bitcast.98), channel_id=1, source_target_pairs={{0,488},{8,496},{16,504},{24,0},{32,8},{40,16},{48,24},{56,32},{64... | collective-permute-start | bytes 98312 | tf_op jit(solution)/shard_map/ppermute | solution.py:16
  241.9 13.9 %collective-permute-start.12 = (bf16[2,16,512]{2,1,0:T(8,128)(2,1)S(1)}, bf16[2,16,512]{2,1,0:T(8,128)(2,1)S(1)}, u32[]{:S(2)}, u32[]{:S(2)}) collective-permute-start(bf16[2,16,512]{2,1,0:T(8,128)(2,1)S(1)} %bitcast.97), channel_id=1, source_target_pairs={{0,480},{8,488},{16,496},{24,504},{32,0},{40,8},{48,16},{56,24},{6... | collective-permute-start | bytes 98312 | tf_op jit(solution)/shard_map/ppermute | solution.py:16
  246.8 9.1 %collective-permute-start.13 = (bf16[2,16,512]{2,1,0:T(8,128)(2,1)S(1)}, bf16[2,16,512]{2,1,0:T(8,128)(2,1)S(1)}, u32[]{:S(2)}, u32[]{:S(2)}) collective-permute-start(bf16[2,16,512]{2,1,0:T(8,128)(2,1)S(1)} %bitcast.96), channel_id=1, source_target_pairs={{0,472},{8,480},{16,488},{24,496},{32,504},{40,0},{48,8},{56,16},{... | collective-permute-start | bytes 98312 | tf_op jit(solution)/shard_map/ppermute | solution.py:16
  249.2 7.4 %collective-permute-start.14 = (bf16[2,16,512]{2,1,0:T(8,128)(2,1)S(1)}, bf16[2,16,512]{2,1,0:T(8,128)(2,1)S(1)}, u32[]{:S(2)}, u32[]{:S(2)}) collective-permute-start(bf16[2,16,512]{2,1,0:T(8,128)(2,1)S(1)} %bitcast.95), channel_id=1, source_target_pairs={{0,464},{8,472},{16,480},{24,488},{32,496},{40,504},{48,0},{56,8},... | collective-permute-start | bytes 98312 | tf_op jit(solution)/shard_map/ppermute | solution.py:16
  253.9 6.1 %collective-permute-start.15 = (bf16[2,16,512]{2,1,0:T(8,128)(2,1)S(1)}, bf16[2,16,512]{2,1,0:T(8,128)(2,1)S(1)}, u32[]{:S(2)}, u32[]{:S(2)}) collective-permute-start(bf16[2,16,512]{2,1,0:T(8,128)(2,1)S(1)} %bitcast.94), channel_id=1, source_target_pairs={{0,456},{8,464},{16,472},{24,480},{32,488},{40,496},{48,504},{56,0... | collective-permute-start | bytes 98312 | tf_op jit(solution)/shard_map/ppermute | solution.py:16
  349.6 5.6 %copy-start.9 = (bf16[8,3,256]{2,1,0:T(4,128)(2,1)S(1)}, bf16[8,3,256]{2,1,0:T(4,128)(2,1)}, u32[]{:S(2)}) copy-start(bf16[8,3,256]{2,1,0:T(4,128)(2,1)} %copy-done.8) | copy-start | bytes 36868
Sparse Core Ops, SparseCore 0:
  11.4 86.2 all-gather.7
  101.0 80.6 all-gather.5
  185.0 80.5 all-gather.9
  268.8 80.7 all-gather.11
  353.3 39.1 reduce-scatter.1
where the time goes:
time: 402 us; the launch traced here: 401 us
  waiting for transfers between devices  209 us (52%)
  blocking collectives  72.5 us (18%)
  starting transfers between devices  46.9 us (12%)
  matrix products  27.8 us (7%)
  local copies, waits for them, and re-layouts  19.2 us (5%)
  between operations  14.7 us (4%)
  other arithmetic  10.6 us (3%)
    all_gather x1, waiting for transfers between devices, project_in(): lax.all_gather(x_weight, 'req', axis=0, tiled=True)  82.5 us
    all_gather x1, waiting for transfers between devices, finish(): lax.all_gather(out_weight, 'req', axis=1, tiled=True)  63.5 us
    all_gather x1, blocking collectives, project_in(): lax.all_gather(step_weight, 'req', axis=0, tiled=True)  55.4 us
    ppermute x16, starting transfers between devices, from_behind(): return lax.ppermute(value, axis, pairs)  46.7 us
    reduce_scatter x1, waiting for transfers between devices, finish(): lax.psum_scatter(terms, 'mdl', scatter_dimension=1, tiled=True)  26 us
    all_gather x1, waiting for transfers between devices, project_in(): lax.all_gather(state_proj, 'req', axis=0, tiled=True)  24.6 us
    psum x1, blocking collectives, finish(): squares = lax.psum(jnp.sum(gated * gated, axis=1), 'mdl')  17.2 us
  transfers between devices with their start and end apart: 21, of which 9 were waited for; matrix products, arithmetic and copies ran while one was open for 13% of the time, Pallas kernels for 0%

commit v1 on v0

--- a/solution.py
+++ b/solution.py
@@ -49,7 +49,9 @@
         lax.all_gather(z_weight, "req", axis=0, tiled=True),
         lax.all_gather(x_weight, "req", axis=0, tiled=True),
         lax.all_gather(state_proj, "req", axis=0, tiled=True),
-        lax.all_gather(step_weight, "req", axis=0, tiled=True),
+        jnp.concatenate(
+            lax.all_to_all(jnp.stack([step_weight] * lax.axis_size("req")), "req", 0, 0), axis=0
+        ),
     )
     gate_pre, inner_raw, state_full, step_raw = tuple(
         (jnp.dot(rows, piece, preferred_element_type=jnp.float32) for piece in pieces)

time: 402 us -> 402 us (level)
  the two profiles are of different devices: /device:TPU:4 before, /device:TPU:6 now
where the time goes in v1:
time: 402 us; the launch traced here: 400 us
  waiting for transfers between devices  249 us (62%)
  starting transfers between devices  60.6 us (15%)
  matrix products  27.9 us (7%)
  local copies, waits for them, and re-layouts  20.8 us (5%)
  blocking collectives  17.2 us (4%)
  between operations  14.7 us (4%)
  other arithmetic  10.6 us (3%)
    all_gather x1, waiting for transfers between devices, project_in(): lax.all_gather(x_weight, 'req', axis=0, tiled=True)  82.5 us
    all_gather x1, waiting for transfers between devices, project_in(): lax.all_gather(state_proj, 'req', axis=0, tiled=True)  64.5 us
    all_gather x1, waiting for transfers between devices, finish(): lax.all_gather(out_weight, 'req', axis=1, tiled=True)  63.4 us
    ppermute x16, starting transfers between devices, from_behind(): return lax.ppermute(value, axis, pairs)  46.6 us
    reduce_scatter x1, waiting for transfers between devices, finish(): lax.psum_scatter(terms, 'mdl', scatter_dimension=1, tiled=True)  26 us
    psum x1, blocking collectives, finish(): squares = lax.psum(jnp.sum(gated * gated, axis=1), 'mdl')  17.2 us
    all_to_all x1, starting transfers between devices, project_in(): lax.all_to_all(jnp.stack([step_weight] * lax.axis_size('req')), 'req', 0, 0)  13.8 us
  transfers between devices with their start and end apart: 22, of which 10 were waited for; matrix products, arithmetic and copies ran while one was open for 13% of the time, Pallas kernels for 0%

profile of v1, /device:TPU:6, one launch (start us, length us, event | category | flops | bytes accessed | tf_op | source)
XLA Modules:
  0.0 400.5 jit_solution(4620947415834880086)
XLA Ops:
  10.1 0.7 reshape.257
  10.8 13.8 %all-to-all-start = ((bf16[64,2,128]{2,1,0:T(2,128)(2,1)}), bf16[64,2,128]{2,1,0:T(2,128)(2,1)S(1)}, u32[]{:S(2)}, u32[]{:S(2)}) async-start(bf16[64,2,128]{2,1,0:T(2,128)(2,1)} %reshape.257), calls=%async_computation | async-start | bytes 65536 | tf_op jit(solution)/shard_map/all_to_all | solution.py:53
  25.3 0.8 reshape.224
  27.9 0.9 select_reduce_fusion.1
  33.2 64.5 %all-gather.7.cloned.1.call-done = bf16[2048,256]{1,0:T(8,128)(2,1)} async-done(((bf16[32,256]{1,0:T(8,128)(2,1)}), bf16[2048,256]{1,0:T(8,128)(2,1)}) %all-gather.7.cloned.1.call-update) | async-done | bytes 1048592 | tf_op jit(solution)/shard_map/all_gather | solution.py:51
  97.6 1.5 convolution_convert_fusion.6
  99.2 82.5 %all-gather.5.cloned.1.call-done = bf16[2048,512]{1,0:T(8,128)(2,1)} async-done(((bf16[32,512]{1,0:T(8,128)(2,1)}), bf16[2048,512]{1,0:T(8,128)(2,1)}) %all-gather.5.cloned.1.call-update) | async-done | bytes 2097168 | tf_op jit(solution)/shard_map/all_gather | solution.py:50
  181.6 2.0 convolution_convert_fusion.5
  186.8 2.2 collective-permute-start.1
  189.1 3.4 collective-permute-start.2
  192.7 3.3 collective-permute-start.3
  196.2 5.2 %collective-permute-start.4 = (bf16[2,16,776]{2,1,0:T(8,128)(2,1)S(1)}, bf16[2,16,776]{2,1,0:T(8,128)(2,1)S(1)}, u32[]{:S(2)}, u32[]{:S(2)}) collective-permute-start(bf16[2,16,776]{2,1,0:T(8,128)(2,1)S(1)} %slice.151), channel_id=1, source_target_pairs={{0,32},{8,40},{16,48},{24,56},{32,64},{40,72},{48,80},{56,88},{64,... | collective-permute-start | bytes 149000 | tf_op jit(solution)/shard_map/ppermute | solution.py:16
  201.9 2.3 collective-permute-start.5
  204.2 3.3 collective-permute-start.6
  207.5 3.2 collective-permute-start.7
  211.5 2.8 collective-permute-done.7
  217.5 0.7 slice.209
  218.2 0.9 fusion.29
  219.7 1.1 reshape.229
  220.9 5.8 %convolution_multiply_fusion = f32[8,16,8,64]{3,1,2,0:T(8,128)S(1)} fusion(f32[8,8,64,128]{3,2,1,0:T(8,128)S(1)} %copy-done.1, f32[8,16,8]{1,2,0:T(8,128)} %copy.153, f32[8,16,768]{2,1,0:T(8,128)S(1)} %divide_multiply_fusion), kind=kOutput, calls=%fused_computation.9 | convolution fusion | flops 100728832 | bytes 2428928 | tf_op jit(solution)/shard_map/stn,shpn->sthp/dot_general | solution.py:89
  226.8 0.7 select_multiply_fusion
  227.5 0.9 fusion.3
  228.4 0.8 copy.155
  229.2 1.9 convert_element_type.68
  231.1 1.2 convolution_convert_fusion.2
  232.6 3.6 collective-permute-start.9
  236.2 3.6 collective-permute-start.10
  239.8 2.0 collective-permute-start.11
  241.8 4.0 %collective-permute-start.12 = (bf16[2,16,512]{2,1,0:T(8,128)(2,1)S(1)}, bf16[2,16,512]{2,1,0:T(8,128)(2,1)S(1)}, u32[]{:S(2)}, u32[]{:S(2)}) collective-permute-start(bf16[2,16,512]{2,1,0:T(8,128)(2,1)S(1)} %bitcast.100), channel_id=1, source_target_pairs={{0,480},{8,488},{16,496},{24,504},{32,0},{40,8},{48,16},{56,24},{6... | collective-permute-start | bytes 98312 | tf_op jit(solution)/shard_map/ppermute | solution.py:16
  245.9 4.3 %collective-permute-start.13 = (bf16[2,16,512]{2,1,0:T(8,128)(2,1)S(1)}, bf16[2,16,512]{2,1,0:T(8,128)(2,1)S(1)}, u32[]{:S(2)}, u32[]{:S(2)}) collective-permute-start(bf16[2,16,512]{2,1,0:T(8,128)(2,1)S(1)} %bitcast.99), channel_id=1, source_target_pairs={{0,472},{8,480},{16,488},{24,496},{32,504},{40,0},{48,8},{56,16},{... | collective-permute-start | bytes 98312 | tf_op jit(solution)/shard_map/ppermute | solution.py:16
  250.3 1.9 collective-permute-start.14
  252.2 4.2 %collective-permute-start.15 = (bf16[2,16,512]{2,1,0:T(8,128)(2,1)S(1)}, bf16[2,16,512]{2,1,0:T(8,128)(2,1)S(1)}, u32[]{:S(2)}, u32[]{:S(2)}) collective-permute-start(bf16[2,16,512]{2,1,0:T(8,128)(2,1)S(1)} %bitcast.97), channel_id=1, source_target_pairs={{0,456},{8,464},{16,472},{24,480},{32,488},{40,496},{48,504},{56,0... | collective-permute-start | bytes 98312 | tf_op jit(solution)/shard_map/ppermute | solution.py:16
  257.0 1.5 collective-permute-done.15
  258.6 0.9 fusion
  259.5 1.7 reshape.233
  261.2 4.4 %all-gather.9.cloned.1.call-done = bf16[2048,512]{1,0:T(8,128)(2,1)} async-done(((bf16[32,512]{1,0:T(8,128)(2,1)}), bf16[2048,512]{1,0:T(8,128)(2,1)}) %all-gather.9.cloned.1.call-update) | async-done | bytes 2097168 | tf_op jit(solution)/shard_map/all_gather | solution.py:49
  265.7 2.8 multiply_reduce_fusion
  268.4 17.2 %psum.7 = f32[128]{0:T(128)S(1)} all-reduce(f32[128]{0:T(128)S(1)} %get-tuple-element.29), channel_id=1, replica_groups=mesh['req'=64,'mdl'=8] {'mdl'}, use_global_device_ids=true, to_apply=%region_5.6 | all-reduce | flops 128 | bytes 1024 | tf_op jit(solution)/shard_map/psum | solution.py:115
  286.1 63.4 %all-gather.11.cloned.1.call-done = bf16[512,2048]{0,1:T(8,128)(2,1)} async-done(((bf16[512,32]{0,1:T(8,128)(2,1)}), bf16[512,2048]{0,1:T(8,128)(2,1)}) %all-gather.11.cloned.1.call-update) | async-done | bytes 2097168 | tf_op jit(solution)/shard_map/all_gather | solution.py:121
  349.6 3.6 fusion.23
  353.8 1.3 exp.41
  355.1 1.2 fusion.4
  356.3 0.8 convolution_convert_fusion.4
  358.3 1.5 copy.158
  359.7 1.0 broadcast_multiply_fusion
  360.8 5.6 %multiply_add_fusion = f32[8,8,64,128]{3,2,1,0:T(8,128)} fusion(f32[8,8,64,128]{3,2,1,0:T(8,128)S(1)} %copy-done.1, f32[8,8]{1,0:T(8,128)} %exp.41, f32[8,16,8,64]{3,2,1,0:T(8,128)S(1)} %broadcast_multiply_fusion, f32[8,16,768]{2,1,0:T(8,128)S(1)} %divide_multiply_fusion), kind=kOutput, calls=%fused_computation.8 | convolution fusion | flops 101711872 | bytes 4784384 | tf_op jit(solution)/shard_map/suh,suhp,sun->shpn/dot_general | solution.py:98
  366.4 26.0 %reduce-scatter.2.cloned.1.call-done = f32[128,256]{1,0:T(8,128)} async-done(((f32[128,2048]{1,0:T(8,128)}), f32[128,256]{1,0:T(8,128)}) %reduce-scatter.2.cloned.1.call-update) | async-done | bytes 131088 | tf_op jit(solution)/shard_map/reduce_scatter | solution.py:124
  392.4 1.5 convert_element_type.74
  (160 shorter events, 21.5 us)
Async XLA Ops:
  7.2 25.6 %copy-start = (bf16[128,2048]{1,0:T(8,128)(2,1)S(1)}, bf16[128,2048]{1,0:T(8,128)(2,1)}, u32[]{:S(2)}) copy-start(bf16[128,2048]{1,0:T(8,128)(2,1)} %param.19) | copy-start | bytes 1572868
  7.2 90.4 %all-gather.7.cloned.1.call-start = ((), (), s32[]{:S(2)}) async-start(), calls=%async_computation.3 | async-start | bytes 1064960 | tf_op jit(solution)/shard_map/all_gather | solution.py:51
  7.9 173.7 %all-gather.5.cloned.1.call-start = ((), (), s32[]{:S(2)}) async-start(), calls=%async_computation.2 | async-start | bytes 2129920 | tf_op jit(solution)/shard_map/all_gather | solution.py:50
  8.7 257.0 %all-gather.9.cloned.1.call-start = ((), (), s32[]{:S(2)}) async-start(), calls=%async_computation.4 | async-start | bytes 2129920 | tf_op jit(solution)/shard_map/all_gather | solution.py:49
  10.8 21.6 %all-to-all-start = ((bf16[64,2,128]{2,1,0:T(2,128)(2,1)}), bf16[64,2,128]{2,1,0:T(2,128)(2,1)S(1)}, u32[]{:S(2)}, u32[]{:S(2)}) async-start(bf16[64,2,128]{2,1,0:T(2,128)(2,1)} %reshape.257), calls=%async_computation | async-start | bytes 65536 | tf_op jit(solution)/shard_map/all_to_all | solution.py:53
  24.7 324.9 %all-gather.11.cloned.1.call-start = ((), (), s32[]{:S(2)}) async-start(), calls=%async_computation.5 | async-start | bytes 2129920 | tf_op jit(solution)/shard_map/all_gather | solution.py:121
  25.2 367.1 %reduce-scatter.2.cloned.1.call-start = ((), (), s32[]{:S(2)}) async-start(), calls=%async_computation.6 | async-start | bytes 1179648 | tf_op jit(solution)/shard_map/reduce_scatter | solution.py:124
  28.8 3.6 copy-start.16
  28.8 3.6 copy-start.17
  28.8 186.0 %copy-start.13 = (s32[8]{0:T(128)}, s32[8]{0:T(128)S(1)}, u32[]{:S(2)}) copy-start(s32[8]{0:T(128)S(1)} %get-tuple-element.10) | copy-start | bytes 100
  32.4 151.6 %copy-start.11 = (s32[8]{0:T(128)}, s32[8]{0:T(128)S(1)}, u32[]{:S(2)}) copy-start(s32[8]{0:T(128)S(1)} %dynamic-slice_reduce_fusion) | copy-start | bytes 100
  99.2 86.1 %copy-start.3 = (bf16[8,3,256]{2,0,1:T(8,128)(2,1)S(1)}, bf16[8,3,256]{2,0,1:T(8,128)(2,1)}, u32[]{:S(2)}) copy-start(bf16[8,3,256]{2,0,1:T(8,128)(2,1)} %param.33) | copy-start | bytes 36868
  99.2 86.7 %copy-start.2 = (bf16[8,3,512]{2,0,1:T(8,128)(2,1)S(1)}, bf16[8,3,512]{2,0,1:T(8,128)(2,1)}, u32[]{:S(2)}) copy-start(bf16[8,3,512]{2,0,1:T(8,128)(2,1)} %param.32) | copy-start | bytes 73732
  184.7 17.2 %collective-permute-start = (bf16[2,16,776]{2,1,0:T(8,128)(2,1)S(1)}, bf16[2,16,776]{2,1,0:T(8,128)(2,1)S(1)}, u32[]{:S(2)}, u32[]{:S(2)}) collective-permute-start(bf16[2,16,776]{2,1,0:T(8,128)(2,1)S(1)} %slice.143), channel_id=1, source_target_pairs={{0,0},{8,8},{16,16},{24,24},{32,32},{40,40},{48,48},{56,56},{64,64... | collective-permute-start | bytes 149000 | tf_op jit(solution)/shard_map/ppermute | solution.py:16
  185.9 31.2 %copy-start.8 = (bf16[8,3,256]{2,1,0:T(4,128)(2,1)}, bf16[8,3,256]{2,1,0:T(4,128)(2,1)S(1)}, u32[]{:S(2)}) copy-start(bf16[8,3,256]{2,1,0:T(4,128)(2,1)S(1)} %copy.145) | copy-start | bytes 36868
  186.6 29.0 %copy-start.14 = (f32[8]{0:T(128)S(1)}, f32[8]{0:T(128)}, u32[]{:S(2)}) copy-start(f32[8]{0:T(128)} %param.24) | copy-start | bytes 100
  186.6 30.5 %copy-start.6 = (bf16[8,3,512]{2,1,0:T(4,128)(2,1)}, bf16[8,3,512]{2,1,0:T(4,128)(2,1)S(1)}, u32[]{:S(2)}) copy-start(bf16[8,3,512]{2,1,0:T(4,128)(2,1)S(1)} %copy.144) | copy-start | bytes 73732
  186.8 17.4 %collective-permute-start.1 = (bf16[2,16,776]{2,1,0:T(8,128)(2,1)S(1)}, bf16[2,16,776]{2,1,0:T(8,128)(2,1)S(1)}, u32[]{:S(2)}, u32[]{:S(2)}) collective-permute-start(bf16[2,16,776]{2,1,0:T(8,128)(2,1)S(1)} %slice.145), channel_id=1, source_target_pairs={{0,8},{8,16},{16,24},{24,32},{32,40},{40,48},{48,56},{56,64},{64,7... | collective-permute-start | bytes 149000 | tf_op jit(solution)/shard_map/ppermute | solution.py:16
  189.1 18.4 %collective-permute-start.2 = (bf16[2,16,776]{2,1,0:T(8,128)(2,1)S(1)}, bf16[2,16,776]{2,1,0:T(8,128)(2,1)S(1)}, u32[]{:S(2)}, u32[]{:S(2)}) collective-permute-start(bf16[2,16,776]{2,1,0:T(8,128)(2,1)S(1)} %slice.147), channel_id=1, source_target_pairs={{0,16},{8,24},{16,32},{24,40},{32,48},{40,56},{48,64},{56,72},{64,... | collective-permute-start | bytes 149000 | tf_op jit(solution)/shard_map/ppermute | solution.py:16
  192.7 18.0 %collective-permute-start.3 = (bf16[2,16,776]{2,1,0:T(8,128)(2,1)S(1)}, bf16[2,16,776]{2,1,0:T(8,128)(2,1)S(1)}, u32[]{:S(2)}, u32[]{:S(2)}) collective-permute-start(bf16[2,16,776]{2,1,0:T(8,128)(2,1)S(1)} %slice.149), channel_id=1, source_target_pairs={{0,24},{8,32},{16,40},{24,48},{32,56},{40,64},{48,72},{56,80},{64,... | collective-permute-start | bytes 149000 | tf_op jit(solution)/shard_map/ppermute | solution.py:16
  196.2 14.7 %collective-permute-start.4 = (bf16[2,16,776]{2,1,0:T(8,128)(2,1)S(1)}, bf16[2,16,776]{2,1,0:T(8,128)(2,1)S(1)}, u32[]{:S(2)}, u32[]{:S(2)}) collective-permute-start(bf16[2,16,776]{2,1,0:T(8,128)(2,1)S(1)} %slice.151), channel_id=1, source_target_pairs={{0,32},{8,40},{16,48},{24,56},{32,64},{40,72},{48,80},{56,88},{64,... | collective-permute-start | bytes 149000 | tf_op jit(solution)/shard_map/ppermute | solution.py:16
  201.9 8.9 %collective-permute-start.5 = (bf16[2,16,776]{2,1,0:T(8,128)(2,1)S(1)}, bf16[2,16,776]{2,1,0:T(8,128)(2,1)S(1)}, u32[]{:S(2)}, u32[]{:S(2)}) collective-permute-start(bf16[2,16,776]{2,1,0:T(8,128)(2,1)S(1)} %slice.153), channel_id=1, source_target_pairs={{0,40},{8,48},{16,56},{24,64},{32,72},{40,80},{48,88},{56,96},{64,... | collective-permute-start | bytes 149000 | tf_op jit(solution)/shard_map/ppermute | solution.py:16
  204.2 7.3 %collective-permute-start.6 = (bf16[2,16,776]{2,1,0:T(8,128)(2,1)S(1)}, bf16[2,16,776]{2,1,0:T(8,128)(2,1)S(1)}, u32[]{:S(2)}, u32[]{:S(2)}) collective-permute-start(bf16[2,16,776]{2,1,0:T(8,128)(2,1)S(1)} %slice.155), channel_id=1, source_target_pairs={{0,48},{8,56},{16,64},{24,72},{32,80},{40,88},{48,96},{56,104},{64... | collective-permute-start | bytes 149000 | tf_op jit(solution)/shard_map/ppermute | solution.py:16
  207.5 6.8 %collective-permute-start.7 = (bf16[2,16,776]{2,1,0:T(8,128)(2,1)S(1)}, bf16[2,16,776]{2,1,0:T(8,128)(2,1)S(1)}, u32[]{:S(2)}, u32[]{:S(2)}) collective-permute-start(bf16[2,16,776]{2,1,0:T(8,128)(2,1)S(1)} %slice.157), channel_id=1, source_target_pairs={{0,56},{8,64},{16,72},{24,80},{32,88},{40,96},{48,104},{56,112},{6... | collective-permute-start | bytes 149000 | tf_op jit(solution)/shard_map/ppermute | solution.py:16
  215.4 1.8 copy-start.4
  217.1 3.7 copy-start.1
  220.8 5.8 %copy-start.5 = (f32[8,16,8]{1,2,0:T(8,128)S(1)}, f32[8,16,8]{1,2,0:T(8,128)}, u32[]{:S(2)}) copy-start(f32[8,16,8]{1,2,0:T(8,128)} %copy.150) | copy-start | bytes 12292
  220.8 5.8 %copy-start.20 = (pred[8,16]{1,0:T(8,128)(4,1)S(1)}, pred[8,16]{1,0:T(8,128)(4,1)}, u32[]{:S(2)}) copy-start(pred[8,16]{1,0:T(8,128)(4,1)} %iota_compare_fusion.9) | copy-start | bytes 388
  220.9 5.9 %copy-start.15 = (f32[8]{0:T(128)S(1)}, f32[8]{0:T(128)}, u32[]{:S(2)}) copy-start(f32[8]{0:T(128)} %param.24) | copy-start | bytes 100
  220.9 5.9 %copy-start.19 = (pred[8,16]{1,0:T(8,128)(4,1)S(1)}, pred[8,16]{1,0:T(8,128)(4,1)}, u32[]{:S(2)}) copy-start(pred[8,16]{1,0:T(8,128)(4,1)} %iota_compare_fusion.8) | copy-start | bytes 388
  220.9 6.6 %copy-start.7 = (f32[8,16,16]{2,1,0:T(8,128)S(1)}, f32[8,16,16]{2,1,0:T(8,128)}, u32[]{:S(2)}) copy-start(f32[8,16,16]{2,1,0:T(8,128)} %fusion.29) | copy-start | bytes 24580
  220.9 6.6 %copy-start.18 = (pred[16,16]{1,0:T(8,128)(4,1)S(1)}, pred[16,16]{1,0:T(8,128)(4,1)}, u32[]{:S(2)}) copy-start(pred[16,16]{1,0:T(8,128)(4,1)} %iota_compare_fusion.3) | copy-start | bytes 772
  220.9 6.6 %copy-start.21 = (f32[8]{0:T(128)S(1)}, f32[8]{0:T(128)}, u32[]{:S(2)}) copy-start(f32[8]{0:T(128)} %param.26) | copy-start | bytes 100
  226.8 0.7 copy-start.10
  228.4 30.2 %copy-start.12 = (s32[8]{0:T(128)S(1)}, s32[8]{0:T(128)}, u32[]{:S(2)}) copy-start(s32[8]{0:T(128)} %copy-done.11) | copy-start | bytes 100
  232.5 13.4 %collective-permute-start.8 = (bf16[2,16,512]{2,1,0:T(8,128)(2,1)S(1)}, bf16[2,16,512]{2,1,0:T(8,128)(2,1)S(1)}, u32[]{:S(2)}, u32[]{:S(2)}) collective-permute-start(bf16[2,16,512]{2,1,0:T(8,128)(2,1)S(1)} %bitcast.104), channel_id=1, source_target_pairs={{0,0},{8,8},{16,16},{24,24},{32,32},{40,40},{48,48},{56,56},{64,64... | collective-permute-start | bytes 98312 | tf_op jit(solution)/shard_map/ppermute | solution.py:16
  232.6 17.7 %collective-permute-start.9 = (bf16[2,16,512]{2,1,0:T(8,128)(2,1)S(1)}, bf16[2,16,512]{2,1,0:T(8,128)(2,1)S(1)}, u32[]{:S(2)}, u32[]{:S(2)}) collective-permute-start(bf16[2,16,512]{2,1,0:T(8,128)(2,1)S(1)} %bitcast.103), channel_id=1, source_target_pairs={{0,504},{8,0},{16,8},{24,16},{32,24},{40,32},{48,40},{56,48},{64,5... | collective-permute-start | bytes 98312 | tf_op jit(solution)/shard_map/ppermute | solution.py:16
  236.2 16.0 %collective-permute-start.10 = (bf16[2,16,512]{2,1,0:T(8,128)(2,1)S(1)}, bf16[2,16,512]{2,1,0:T(8,128)(2,1)S(1)}, u32[]{:S(2)}, u32[]{:S(2)}) collective-permute-start(bf16[2,16,512]{2,1,0:T(8,128)(2,1)S(1)} %bitcast.102), channel_id=1, source_target_pairs={{0,496},{8,504},{16,0},{24,8},{32,16},{40,24},{48,32},{56,40},{64,... | collective-permute-start | bytes 98312 | tf_op jit(solution)/shard_map/ppermute | solution.py:16
  239.8 16.6 %collective-permute-start.11 = (bf16[2,16,512]{2,1,0:T(8,128)(2,1)S(1)}, bf16[2,16,512]{2,1,0:T(8,128)(2,1)S(1)}, u32[]{:S(2)}, u32[]{:S(2)}) collective-permute-start(bf16[2,16,512]{2,1,0:T(8,128)(2,1)S(1)} %bitcast.101), channel_id=1, source_target_pairs={{0,488},{8,496},{16,504},{24,0},{32,8},{40,16},{48,24},{56,32},{64... | collective-permute-start | bytes 98312 | tf_op jit(solution)/shard_map/ppermute | solution.py:16
  241.8 14.7 %collective-permute-start.12 = (bf16[2,16,512]{2,1,0:T(8,128)(2,1)S(1)}, bf16[2,16,512]{2,1,0:T(8,128)(2,1)S(1)}, u32[]{:S(2)}, u32[]{:S(2)}) collective-permute-start(bf16[2,16,512]{2,1,0:T(8,128)(2,1)S(1)} %bitcast.100), channel_id=1, source_target_pairs={{0,480},{8,488},{16,496},{24,504},{32,0},{40,8},{48,16},{56,24},{6... | collective-permute-start | bytes 98312 | tf_op jit(solution)/shard_map/ppermute | solution.py:16
  245.9 10.6 %collective-permute-start.13 = (bf16[2,16,512]{2,1,0:T(8,128)(2,1)S(1)}, bf16[2,16,512]{2,1,0:T(8,128)(2,1)S(1)}, u32[]{:S(2)}, u32[]{:S(2)}) collective-permute-start(bf16[2,16,512]{2,1,0:T(8,128)(2,1)S(1)} %bitcast.99), channel_id=1, source_target_pairs={{0,472},{8,480},{16,488},{24,496},{32,504},{40,0},{48,8},{56,16},{... | collective-permute-start | bytes 98312 | tf_op jit(solution)/shard_map/ppermute | solution.py:16
  250.3 6.7 %collective-permute-start.14 = (bf16[2,16,512]{2,1,0:T(8,128)(2,1)S(1)}, bf16[2,16,512]{2,1,0:T(8,128)(2,1)S(1)}, u32[]{:S(2)}, u32[]{:S(2)}) collective-permute-start(bf16[2,16,512]{2,1,0:T(8,128)(2,1)S(1)} %bitcast.98), channel_id=1, source_target_pairs={{0,464},{8,472},{16,480},{24,488},{32,496},{40,504},{48,0},{56,8},... | collective-permute-start | bytes 98312 | tf_op jit(solution)/shard_map/ppermute | solution.py:16
  252.2 6.2 %collective-permute-start.15 = (bf16[2,16,512]{2,1,0:T(8,128)(2,1)S(1)}, bf16[2,16,512]{2,1,0:T(8,128)(2,1)S(1)}, u32[]{:S(2)}, u32[]{:S(2)}) collective-permute-start(bf16[2,16,512]{2,1,0:T(8,128)(2,1)S(1)} %bitcast.97), channel_id=1, source_target_pairs={{0,456},{8,464},{16,472},{24,480},{32,488},{40,496},{48,504},{56,0... | collective-permute-start | bytes 98312 | tf_op jit(solution)/shard_map/ppermute | solution.py:16
  349.6 5.6 %copy-start.9 = (bf16[8,3,256]{2,1,0:T(4,128)(2,1)S(1)}, bf16[8,3,256]{2,1,0:T(4,128)(2,1)}, u32[]{:S(2)}) copy-start(bf16[8,3,256]{2,1,0:T(4,128)(2,1)} %copy-done.8) | copy-start | bytes 36868
Sparse Core Ops, SparseCore 0:
  11.4 86.2 all-gather.6
  101.0 80.6 all-gather.4
  185.0 80.6 all-gather.8
  268.9 80.6 all-gather.10
  353.3 39.0 reduce-scatter.1
